TPU v7x, 32 devices: a whole 2x2x4 slice. The times are simulated.
32 devices in a mesh: grp: 2 (over y), seq: 16 (over z, x, core).
Axes of the slice: x: 2, y: 2, z: 4, core: 2. Of those that a mesh axis runs over, the one named last changes fastest.
Arguments:
- query: bfloat16 [2, 16, 1024, 128], P('grp', None, 'seq'), parts along dimension 0, may hold values from -49 to 49
- key: bfloat16 [2, 16, 1024, 128], P('grp', None, 'seq'), parts along dimension 0, may hold values from -8 to 8
- value: bfloat16 [2, 16, 1024, 128], P('grp', None, 'seq'), parts along dimension 0, may hold values from -6 to 6
- mem_key: bfloat16 [2, 16, 1024, 128], P('grp', None, 'seq'), parts along dimension 0, may hold values from -8 to 8
- mem_value: bfloat16 [2, 16, 1024, 128], P('grp', None, 'seq'), parts along dimension 0, may hold values from -6 to 6
- mem_count: int32 [2, 4], P('grp'), parts along dimension 0, may hold values from 1 to 256, as said below
- mem_factor: int32 [2, 4], P('grp'), parts along dimension 0, may hold values from 1 to 16, as said below
- out_weight: bfloat16 [2048, 3072], P('seq'), may hold values from -0.125 to 0.125
Outputs:
- block_out: bfloat16 [2, 1024, 3072], P('grp', 'seq'), parts along dimension 0
There are 2 independent parts, one for each index of `grp`. A program takes and returns all parts, laid end to end along the dimension named above; an argument that names none is the same for every part. Nothing has to cross between parts.
Inputs may be any that keep to these rules, and one draw needn't show every extreme that they name: `mem_count`: some stretch of every sequence holds exactly 256 live tokens. `mem_factor`: powers of two.
All inputs are finite; a program needn't handle non-finite values.
Results may differ from a plain program's by a relative error of at most 0.0052.
Values may be sent and summed in bfloat16 or wider, within the bound.
A program may use at most 128 MiB of HBM per device.

v0:
```python
import jax
import jax.numpy as jnp
from jax import lax
from jax.sharding import PartitionSpec as P

MCAP = 256


def per_device(query, key, value, mem_key, mem_value, mem_count, mem_factor, out_weight):
    seqs, heads, rows, width = query.shape
    slots_dev = mem_key.shape[2]
    devices = lax.axis_size("seq")
    groups = seqs * heads
    copies = devices // groups
    half = rows // copies
    feat = out_weight.shape[1]
    own_queries = (
        query.reshape(groups, half, copies, width)
        .transpose(0, 2, 1, 3)
        .reshape(groups * copies, half, width)
    )

    def spread(array, count):
        widened = jnp.broadcast_to(
            array.reshape(groups, 1, count, width), (groups, copies, count, width)
        )
        return widened.reshape(groups * copies, count, width)

    head_q, head_k, head_v, head_mk, head_mv = (
        lax.all_to_all(own_queries, "seq", split_axis=0, concat_axis=1, tiled=True),
        lax.all_to_all(spread(key, rows), "seq", split_axis=0, concat_axis=1, tiled=True),
        lax.all_to_all(spread(value, rows), "seq", split_axis=0, concat_axis=1, tiled=True),
        lax.all_to_all(spread(mem_key, slots_dev), "seq", split_axis=0, concat_axis=1, tiled=True),
        lax.all_to_all(
            spread(mem_value, slots_dev), "seq", split_axis=0, concat_axis=1, tiled=True
        ),
    )
    length_q = head_q.shape[1]
    length = head_k.shape[1]
    slots = head_mk.shape[1]
    seq_index = lax.axis_index("seq") // copies // heads
    counts = lax.dynamic_index_in_dim(mem_count, seq_index, 0, keepdims=False)
    factors = lax.dynamic_index_in_dim(mem_factor, seq_index, 0, keepdims=False)
    slot = jnp.arange(slots)
    stretch_of = slot // MCAP
    offset = slot % MCAP
    picked = stretch_of[:, None] == jnp.arange(counts.shape[0])[None, :]
    slot_count = jnp.sum(jnp.where(picked, counts[None, :], 0), 1)
    slot_factor = jnp.sum(jnp.where(picked, factors[None, :], 0), 1)
    bias = jnp.where(
        offset < slot_count, jnp.log(slot_factor.astype(jnp.float32)), jnp.float32(-1000000000.0)
    )
    full_bias = jnp.concatenate([jnp.zeros((length,), jnp.float32), bias])
    all_keys = jnp.concatenate([head_k[0], head_mk[0]], 0)
    all_vals = jnp.concatenate([head_v[0], head_mv[0]], 0)
    scale = width ** (-0.5)
    block = min(512, length_q)
    query_blocks = head_q[0].reshape(length_q // block, block, width)

    def attend(queries):
        score = (
            jnp.einsum("qd,kd->qk", queries, all_keys, preferred_element_type=jnp.float32) * scale
        )
        score = score + full_bias[None, :]
        top = jnp.max(score, axis=1, keepdims=True)
        prob = jnp.exp(score - top)
        total = jnp.sum(prob, axis=1, keepdims=True)
        weight = prob.astype(jnp.bfloat16)
        attended = jnp.dot(weight, all_vals, preferred_element_type=jnp.float32) / total
        return attended.astype(jnp.bfloat16)

    attended = lax.map(attend, query_blocks).reshape(1, length_q, width)
    returned = lax.all_to_all(attended, "seq", split_axis=1, concat_axis=0, tiled=True)
    columns = returned.reshape(seqs, heads, copies, half, width).transpose(0, 3, 2, 1, 4)
    columns = columns.reshape(seqs * rows, heads * width)
    mixed = jnp.dot(
        columns,
        lax.all_gather(out_weight, "seq", axis=0, tiled=True),
        preferred_element_type=jnp.float32,
    )
    result = mixed.reshape(seqs, rows, feat).astype(jnp.bfloat16)
    return result


def solution(mesh):
    in_specs = (
        P("grp", None, "seq", None),
        P("grp", None, "seq", None),
        P("grp", None, "seq", None),
        P("grp", None, "seq", None),
        P("grp", None, "seq", None),
        P("grp", None),
        P("grp", None),
        P("seq", None),
    )
    out_specs = P("grp", "seq", None)
    return jax.shard_map(
        per_device, mesh=mesh, in_specs=in_specs, out_specs=out_specs, check_vma=False
    )
```

profile of v0, /device:TPU:0, one launch (start us, length us, event | category | flops | bytes accessed | tf_op | source)
XLA Modules:
  0.0 152.8 jit_solution(13897523027870306095)
XLA Ops:
  6.5 0.0 all-gather.2.cloned.1.call-start
  6.5 0.7 all-gather.2.cloned.1.call-update
  7.3 17.4 %all_to_all.24 = bf16[16,64,128]{2,1,0:T(8,128)(2,1)S(1)} all-to-all(bf16[16,64,128]{2,1,0:T(8,128)(2,1)} %bitcast.58), channel_id=1, replica_groups=mesh['grp'=2,'seq'=16] {'seq'}, dimensions={0} | all-to-all | bytes 524288 | tf_op jit(solution)/shard_map/all_to_all | solution.py:31
  24.7 18.1 %all_to_all.25 = bf16[16,64,128]{2,1,0:T(8,128)(2,1)S(1)} all-to-all(bf16[16,64,128]{2,1,0:T(8,128)(2,1)} %bitcast.59), channel_id=1, replica_groups=mesh['grp'=2,'seq'=16] {'seq'}, dimensions={0} | all-to-all | bytes 524288 | tf_op jit(solution)/shard_map/all_to_all | solution.py:33
  42.8 17.7 %all_to_all.26 = bf16[16,64,128]{2,1,0:T(8,128)(2,1)S(1)} all-to-all(bf16[16,64,128]{2,1,0:T(8,128)(2,1)} %bitcast.60), channel_id=1, replica_groups=mesh['grp'=2,'seq'=16] {'seq'}, dimensions={0} | all-to-all | bytes 524288 | tf_op jit(solution)/shard_map/all_to_all | solution.py:32
  60.5 4.0 %all-to-all-start.4 = ((bf16[16,64,128]{2,1,0:T(8,128)(2,1)}), bf16[16,64,128]{2,1,0:T(8,128)(2,1)S(1)}, u32[]{:S(2)}, u32[]{:S(2)}) async-start(bf16[16,64,128]{2,1,0:T(8,128)(2,1)} %bitcast.61), calls=%async_computation.4 | async-start | bytes 524288 | tf_op jit(solution)/shard_map/all_to_all | solution.py:34
  64.5 0.8 select_reduce_fusion.1
  65.3 13.5 %all-to-all-done.4 = bf16[16,64,128]{2,1,0:T(8,128)(2,1)S(1)} async-done(((bf16[16,64,128]{2,1,0:T(8,128)(2,1)}), bf16[16,64,128]{2,1,0:T(8,128)(2,1)S(1)}, u32[]{:S(2)}, u32[]{:S(2)}) %all-to-all-start.4) | async-done | bytes 262176 | tf_op jit(solution)/shard_map/all_to_all | solution.py:34
  78.8 5.9 %all-to-all-start = ((bf16[16,64,128]{2,1,0:T(8,128)(2,1)}), bf16[16,64,128]{2,1,0:T(8,128)(2,1)S(1)}, u32[]{:S(2)}, u32[]{:S(2)}) async-start(bf16[16,64,128]{2,1,0:T(8,128)(2,1)} %bitcast.62), calls=%async_computation | async-start | bytes 524288 | tf_op jit(solution)/shard_map/all_to_all | solution.py:30
  84.8 14.5 %all-to-all-done = bf16[16,64,128]{2,1,0:T(8,128)(2,1)S(1)} async-done(((bf16[16,64,128]{2,1,0:T(8,128)(2,1)}), bf16[16,64,128]{2,1,0:T(8,128)(2,1)S(1)}, u32[]{:S(2)}, u32[]{:S(2)}) %all-to-all-start) | async-done | bytes 262176 | tf_op jit(solution)/shard_map/all_to_all | solution.py:30
  99.3 5.6 %while.10 = (s32[]{:T(128)}, bf16[2,512,128]{2,1,0:T(8,128)(2,1)S(1)}, bf16[2,512,128]{2,1,0:T(8,128)(2,1)S(1)}, bf16[2048,128]{1,0:T(8,128)(2,1)S(1)}, f32[2048...) while((s32[]{:T(128)}, bf16[2,512,128]{2,1,0:T(8,128)(2,1)S(1)}, ...), condition=%wide.region_5.6_spmd, body=%wide.region_2.5_spmd.sunk | while | flops 548535296 | bytes 13928533 | solution.py:72
  99.3 0.8 fusion.43
  100.1 1.0 fusion.44
  101.0 1.0 fusion.45
  102.1 0.8 fusion.43
  102.9 1.0 fusion.44
  103.8 1.0 fusion.45
  104.9 0.4 copy.22
  105.3 0.5 broadcast.60
  105.8 2.2 %reduce = bf16[1024,128]{1,0:T(8,128)(2,1)S(1)} reduce(bf16[1024,1,128]{2,1,0:T(2,128)(2,1)S(1)} %bitcast.50, bf16[]{:T(256)} %broadcast.60), dimensions={1}, to_apply=%bitcast.39.reduce_sub_computation | reduce | bytes 524290
  108.0 0.1 reshape.54
  108.1 20.1 %all_to_all.27 = bf16[16,2,4096]{2,1,0:T(2,128)(2,1)S(1)} all-to-all(bf16[16,2,4096]{2,1,0:T(2,128)(2,1)S(1)} %reshape.54), channel_id=1, replica_groups=mesh['grp'=2,'seq'=16] {'seq'}, dimensions={0} | all-to-all | bytes 524288 | tf_op jit(solution)/shard_map/all_to_all | solution.py:73
  128.2 0.3 reshape.55
  128.5 0.2 copy.14
  128.7 9.6 %all-gather.2.cloned.1.call-done = bf16[2048,3072]{1,0:T(8,128)(2,1)} async-done(((bf16[128,3072]{1,0:T(8,128)(2,1)}), bf16[2048,3072]{1,0:T(8,128)(2,1)}) %all-gather.2.cloned.1.call-update) | async-done | bytes 12582928 | tf_op jit(solution)/shard_map/all_gather | solution.py:78
  138.3 7.6 %fusion.22 = bf16[1,64,3072]{2,1,0:T(8,128)(2,1)} fusion(bf16[2048,3072]{1,0:T(8,128)(2,1)} %all-gather.2.cloned.1.call-done, bf16[8,8,16,128]{3,2,1,0:T(8,128)(2,1)S(1)} %bitcast.51), kind=kOutput, calls=%fused_computation.16 | convolution fusion | flops 805502976 | bytes 13238272 | tf_op jit(solution)/shard_map/dot_general | solution.py:76
  (7 shorter events, 0.1 us)
Async XLA Ops:
  6.5 131.8 %all-gather.2.cloned.1.call-start = ((), (), s32[]{:S(2)}) async-start(), calls=%async_computation.6 | async-start | bytes 13369344 | tf_op jit(solution)/shard_map/all_gather | solution.py:78
  60.5 18.3 %all-to-all-start.4 = ((bf16[16,64,128]{2,1,0:T(8,128)(2,1)}), bf16[16,64,128]{2,1,0:T(8,128)(2,1)S(1)}, u32[]{:S(2)}, u32[]{:S(2)}) async-start(bf16[16,64,128]{2,1,0:T(8,128)(2,1)} %bitcast.61), calls=%async_computation.4 | async-start | bytes 524288 | tf_op jit(solution)/shard_map/all_to_all | solution.py:34
  78.8 20.5 %all-to-all-start = ((bf16[16,64,128]{2,1,0:T(8,128)(2,1)}), bf16[16,64,128]{2,1,0:T(8,128)(2,1)S(1)}, u32[]{:S(2)}, u32[]{:S(2)}) async-start(bf16[16,64,128]{2,1,0:T(8,128)(2,1)} %bitcast.62), calls=%async_computation | async-start | bytes 524288 | tf_op jit(solution)/shard_map/all_to_all | solution.py:30
Sparse Core Ops, SparseCore 0:
  9.6 128.6 all-gather.1
where the time goes:
time: 154 us; the launch traced here: 153 us
  blocking collectives  73.4 us (48%)
  waiting for transfers between devices  38.3 us (25%)
  between operations  13.5 us (9%)
  matrix products  11.3 us (7%)
  starting transfers between devices  9.82 us (6%)
  other arithmetic  4.96 us (3%)
    all_to_all x1, blocking collectives, per_device(): lax.all_to_all(attended, 'seq', split_axis=1, concat_axis=0, tiled=True)  20.1 us
    all_to_all x1, blocking collectives, per_device(): lax.all_to_all(spread(mem_key, slots_dev), 'seq', split_axis=0, concat_ax...  18.1 us
    all_to_all x1, blocking collectives, per_device(): lax.all_to_all(spread(value, rows), 'seq', split_axis=0, concat_axis=1, t...  17.7 us
    all_to_all x1, blocking collectives, per_device(): lax.all_to_all(spread(key, rows), 'seq', split_axis=0, concat_axis=1, til...  17.4 us
    all_to_all x1, waiting for transfers between devices, per_device(): lax.all_to_all(own_queries, 'seq', split_axis=0, concat_axis=1, tiled=True)  14.5 us
    all_to_all x1, waiting for transfers between devices, per_device(): lax.all_to_all(spread(mem_value, slots_dev), 'seq', split_axis=0, concat_...  13.5 us
    all_gather x1, waiting for transfers between devices, per_device(): lax.all_gather(out_weight, 'seq', axis=0, tiled=True)  9.63 us
    dot_general x1, matrix products, per_device(): jnp.dot(columns, lax.all_gather(out_weight, 'seq', axis=0, tiled=True), p...  7.62 us
  transfers between devices with their start and end apart: 3, of which 3 were waited for; matrix products, arithmetic and copies ran while one was open for 7% of the time, Pallas kernels for 0%

commit v1 on v0

--- a/solution.py
+++ b/solution.py
@@ -31,8 +31,14 @@
         lax.all_to_all(spread(key, rows), "seq", split_axis=0, concat_axis=1, tiled=True),
         lax.all_to_all(spread(value, rows), "seq", split_axis=0, concat_axis=1, tiled=True),
         lax.all_to_all(spread(mem_key, slots_dev), "seq", split_axis=0, concat_axis=1, tiled=True),
-        lax.all_to_all(
-            spread(mem_value, slots_dev), "seq", split_axis=0, concat_axis=1, tiled=True
+        jnp.concatenate(
+            lax.all_to_all(
+                jnp.stack(jnp.split(spread(mem_value, slots_dev), lax.axis_size("seq"), axis=0)),
+                "seq",
+                0,
+                0,
+            ),
+            axis=1,
         ),
     )
     length_q = head_q.shape[1]

time: 154 us -> 160 us (1.039)
  local copies, waits for them, and re-layouts: 1.47 us -> 13 us
  waiting for transfers between devices: 38.3 us -> 29.1 us
  starting transfers between devices: 9.82 us -> 11.5 us
    unnamed x4 -> x19, local copies, waits for them, and re-layouts: 0.88 us -> 11.7 us
    all_gather x1, waiting for transfers between devices: 9.63 us -> 0.02 us  [per_device(): lax.all_gather(out_weight, 'seq', axis=0, tiled=True)]
    all_to_all x1, blocking collectives: 20.1 us -> 15.6 us  [per_device(): lax.all_to_all(attended, 'seq', split_axis=1, concat_axis=0, tiled=True)]
    all_to_all x1, blocking collectives: 18.1 us -> 21.8 us  [per_device(): lax.all_to_all(jnp.stack(jnp.split(spread(mem_value, slots_dev), lax.axis...]
    all_to_all x1, starting transfers between devices: 3.95 us -> 5.86 us  [per_device(): lax.all_to_all(spread(mem_key, slots_dev), 'seq', split_axis=0, concat_ax...]
    all_to_all x1, blocking collectives: 17.7 us -> 19.6 us  [per_device(): lax.all_to_all(spread(value, rows), 'seq', split_axis=0, concat_axis=1, t...]
  transfers between devices with their start and end apart: 3 -> 3, of which waited for: 3 -> 2; matrix products, arithmetic and copies ran while one was open for 7% -> 14% of each run, Pallas kernels for 0% -> 0%
where the time goes in v1:
time: 160 us; the launch traced here: 158 us
  blocking collectives  74.4 us (47%)
  waiting for transfers between devices  29.1 us (18%)
  between operations  13.5 us (8%)
  local copies, waits for them, and re-layouts  13 us (8%)
  starting transfers between devices  11.5 us (7%)
  matrix products  11.3 us (7%)
  other arithmetic  4.96 us (3%)
    all_to_all x1, blocking collectives, per_device(): lax.all_to_all(jnp.stack(jnp.split(spread(mem_value, slots_dev), lax.axis...  21.8 us
    all_to_all x1, blocking collectives, per_device(): lax.all_to_all(spread(value, rows), 'seq', split_axis=0, concat_axis=1, t...  19.6 us
    all_to_all x1, blocking collectives, per_device(): lax.all_to_all(spread(key, rows), 'seq', split_axis=0, concat_axis=1, til...  17.5 us
    all_to_all x1, blocking collectives, per_device(): lax.all_to_all(attended, 'seq', split_axis=1, concat_axis=0, tiled=True)  15.6 us
    all_to_all x1, waiting for transfers between devices, per_device(): lax.all_to_all(own_queries, 'seq', split_axis=0, concat_axis=1, tiled=True)  14.5 us
    all_to_all x1, waiting for transfers between devices, per_device(): lax.all_to_all(spread(mem_key, slots_dev), 'seq', split_axis=0, concat_ax...  13.8 us
    unnamed x19, local copies, waits for them, and re-layouts  11.7 us
    dot_general x1, matrix products, per_device(): jnp.dot(columns, lax.all_gather(out_weight, 'seq', axis=0, tiled=True), p...  7.62 us
  transfers between devices with their start and end apart: 3, of which 2 were waited for; matrix products, arithmetic and copies ran while one was open for 14% of the time, Pallas kernels for 0%

profile of v1, /device:TPU:0, one launch (start us, length us, event | category | flops | bytes accessed | tf_op | source)
XLA Modules:
  0.0 157.8 jit_solution(8750959512103569811)
XLA Ops:
  6.5 0.0 all-gather.2.cloned.1.call-start
  6.5 0.7 all-gather.2.cloned.1.call-update
  7.3 0.7 constant_dynamic-update-slice_fusion.15
  8.0 0.7 constant_dynamic-update-slice_fusion.14
  8.7 0.7 constant_dynamic-update-slice_fusion.13
  9.4 0.7 constant_dynamic-update-slice_fusion.12
  10.2 0.7 constant_dynamic-update-slice_fusion.11
  10.9 0.7 constant_dynamic-update-slice_fusion.10
  11.6 0.7 constant_dynamic-update-slice_fusion.9
  12.3 0.7 constant_dynamic-update-slice_fusion.8
  13.1 0.7 constant_dynamic-update-slice_fusion.7
  13.8 0.7 constant_dynamic-update-slice_fusion.6
  14.5 0.7 constant_dynamic-update-slice_fusion.5
  15.2 0.7 constant_dynamic-update-slice_fusion.4
  15.9 0.7 constant_dynamic-update-slice_fusion.3
  16.7 0.7 constant_dynamic-update-slice_fusion.2
  17.4 0.7 constant_dynamic-update-slice_fusion.1
  18.1 0.7 constant_dynamic-update-slice_fusion
  18.8 21.8 %all_to_all.24 = bf16[16,1,64,128]{3,2,1,0:T(8,128)(2,1)S(1)} all-to-all(bf16[16,1,64,128]{3,2,1,0:T(8,128)(2,1)S(1)} %constant_dynamic-update-slice_fusion), channel_id=1, replica_groups=mesh['grp'=2,'seq'=16] {'seq'}, dimensions={0} | all-to-all | bytes 524288 | tf_op jit(solution)/shard_map/all_to_all | solution.py:35
  40.6 19.6 %all_to_all.25 = bf16[16,64,128]{2,1,0:T(8,128)(2,1)S(1)} all-to-all(bf16[16,64,128]{2,1,0:T(8,128)(2,1)} %bitcast.57), channel_id=1, replica_groups=mesh['grp'=2,'seq'=16] {'seq'}, dimensions={0} | all-to-all | bytes 524288 | tf_op jit(solution)/shard_map/all_to_all | solution.py:32
  60.3 17.5 %all_to_all.52 = bf16[16,64,128]{2,1,0:T(8,128)(2,1)S(1)} all-to-all(bf16[16,64,128]{2,1,0:T(8,128)(2,1)} %bitcast.58), channel_id=1, replica_groups=mesh['grp'=2,'seq'=16] {'seq'}, dimensions={0} | all-to-all | bytes 524288 | tf_op jit(solution)/shard_map/all_to_all | solution.py:31
  77.7 5.9 %all-to-all-start.2 = ((bf16[16,64,128]{2,1,0:T(8,128)(2,1)}), bf16[16,64,128]{2,1,0:T(8,128)(2,1)S(1)}, u32[]{:S(2)}, u32[]{:S(2)}) async-start(bf16[16,64,128]{2,1,0:T(8,128)(2,1)} %bitcast.59), calls=%async_computation.2 | async-start | bytes 524288 | tf_op jit(solution)/shard_map/all_to_all | solution.py:33
  83.6 0.8 select_reduce_fusion.1
  84.4 13.8 %all-to-all-done.2 = bf16[16,64,128]{2,1,0:T(8,128)(2,1)S(1)} async-done(((bf16[16,64,128]{2,1,0:T(8,128)(2,1)}), bf16[16,64,128]{2,1,0:T(8,128)(2,1)S(1)}, u32[]{:S(2)}, u32[]{:S(2)}) %all-to-all-start.2) | async-done | bytes 262176 | tf_op jit(solution)/shard_map/all_to_all | solution.py:33
  98.2 5.6 %all-to-all-start = ((bf16[16,64,128]{2,1,0:T(8,128)(2,1)}), bf16[16,64,128]{2,1,0:T(8,128)(2,1)S(1)}, u32[]{:S(2)}, u32[]{:S(2)}) async-start(bf16[16,64,128]{2,1,0:T(8,128)(2,1)} %bitcast.60), calls=%async_computation | async-start | bytes 524288 | tf_op jit(solution)/shard_map/all_to_all | solution.py:30
  104.0 14.5 %all-to-all-done = bf16[16,64,128]{2,1,0:T(8,128)(2,1)S(1)} async-done(((bf16[16,64,128]{2,1,0:T(8,128)(2,1)}), bf16[16,64,128]{2,1,0:T(8,128)(2,1)S(1)}, u32[]{:S(2)}, u32[]{:S(2)}) %all-to-all-start) | async-done | bytes 262176 | tf_op jit(solution)/shard_map/all_to_all | solution.py:30
  118.5 5.6 %while.10 = (s32[]{:T(128)}, bf16[2,512,128]{2,1,0:T(8,128)(2,1)S(1)}, bf16[2,512,128]{2,1,0:T(8,128)(2,1)S(1)}, bf16[2048,128]{1,0:T(8,128)(2,1)S(1)}, f32[2048...) while((s32[]{:T(128)}, bf16[2,512,128]{2,1,0:T(8,128)(2,1)S(1)}, ...), condition=%wide.region_5.6_spmd, body=%wide.region_2.5_spmd.sunk | while | flops 548535296 | bytes 13928533 | solution.py:78
  118.5 0.8 fusion.43
  119.3 1.0 fusion.44
  120.2 1.0 fusion.45
  121.3 0.8 fusion.43
  122.1 1.0 fusion.44
  123.0 1.0 fusion.45
  124.1 0.4 copy.22
  124.5 0.5 broadcast.60
  125.0 2.2 %reduce = bf16[1024,128]{1,0:T(8,128)(2,1)S(1)} reduce(bf16[1024,1,128]{2,1,0:T(2,128)(2,1)S(1)} %bitcast.49, bf16[]{:T(256)} %broadcast.60), dimensions={1}, to_apply=%bitcast.38.reduce_sub_computation | reduce | bytes 524290
  127.2 0.1 reshape.82
  127.3 15.6 %all_to_all.53 = bf16[16,2,4096]{2,1,0:T(2,128)(2,1)S(1)} all-to-all(bf16[16,2,4096]{2,1,0:T(2,128)(2,1)S(1)} %reshape.82), channel_id=1, replica_groups=mesh['grp'=2,'seq'=16] {'seq'}, dimensions={0} | all-to-all | bytes 524288 | tf_op jit(solution)/shard_map/all_to_all | solution.py:79
  142.8 0.3 reshape.83
  143.2 0.2 copy.14
  143.3 0.0 all-gather.2.cloned.1.call-done
  143.4 7.6 %fusion.22 = bf16[1,64,3072]{2,1,0:T(8,128)(2,1)} fusion(bf16[2048,3072]{1,0:T(8,128)(2,1)} %all-gather.2.cloned.1.call-done, bf16[8,8,16,128]{3,2,1,0:T(8,128)(2,1)S(1)} %bitcast.50), kind=kOutput, calls=%fused_computation.16 | convolution fusion | flops 805502976 | bytes 13238272 | tf_op jit(solution)/shard_map/dot_general | solution.py:82
  (7 shorter events, 0.1 us)
Async XLA Ops:
  6.5 136.8 %all-gather.2.cloned.1.call-start = ((), (), s32[]{:S(2)}) async-start(), calls=%async_computation.6 | async-start | bytes 13369344 | tf_op jit(solution)/shard_map/all_gather | solution.py:84
  77.7 20.5 %all-to-all-start.2 = ((bf16[16,64,128]{2,1,0:T(8,128)(2,1)}), bf16[16,64,128]{2,1,0:T(8,128)(2,1)S(1)}, u32[]{:S(2)}, u32[]{:S(2)}) async-start(bf16[16,64,128]{2,1,0:T(8,128)(2,1)} %bitcast.59), calls=%async_computation.2 | async-start | bytes 524288 | tf_op jit(solution)/shard_map/all_to_all | solution.py:33
  98.2 20.3 %all-to-all-start = ((bf16[16,64,128]{2,1,0:T(8,128)(2,1)}), bf16[16,64,128]{2,1,0:T(8,128)(2,1)S(1)}, u32[]{:S(2)}, u32[]{:S(2)}) async-start(bf16[16,64,128]{2,1,0:T(8,128)(2,1)} %bitcast.60), calls=%async_computation | async-start | bytes 524288 | tf_op jit(solution)/shard_map/all_to_all | solution.py:30
Sparse Core Ops, SparseCore 0:
  9.6 128.0 all-gather.1
